TPU v7x, 256 devices: a whole 4x4x8 slice. The times are simulated.
256 devices in a mesh: grp: 8 (over y, core), pan: 32 (over z, x).
Axes of the slice: x: 4, y: 4, z: 8, core: 2. Of those that a mesh axis runs over, the one named last changes fastest.
Arguments:
- anc_rows: bfloat16 [16384, 16384], P('grp', 'pan'), as said below
- row_home: int32 [128], replicated, may hold values from 0 to 127, as said below
- block_lists: int32 [8, 64], replicated, may hold values from 0 to 127, as said below
- front_blocks: int32 [8], replicated, may hold values from 32 to 64, as said below
- panel: bfloat16 [8, 8192, 768], P('grp', 'pan'), may hold values from -0.29882812 to 0.29882812
- pivot_inverse: bfloat16 [8, 768, 768], P('grp'), as said below
Outputs:
- cross_cov: bfloat16 [8, 8192, 768], P('grp', 'pan')
- pivot_cov: float32 [8, 768, 768], P('grp', 'pan')
Inputs may be any that keep to these rules, and one draw needn't show every extreme that they name: `row_home`: A permutation of 0 to 127; the 4 index blocks of each window [4 q, 4 q + 4) have their storage row blocks in one front group. `block_lists`: rising along each row; entries 2 * q to 2 * q + 1 lie in [4 * q, 4 * q + 4). `front_blocks`: some front has all 64 blocks. `anc_rows`: storage row block row_home[b] holds row block b of a symmetric matrix. `pivot_inverse`: lower triangular.
All inputs are finite; a program needn't handle non-finite values.
Results may differ from a plain program's by a relative error of at most 0.0095.
Values may be sent and summed in bfloat16 or wider, within the bound.
A program may use at most 128 MiB of HBM per device.

v0:
```python
import jax
import jax.numpy as jnp
from jax import lax
from jax.sharding import PartitionSpec as P

BLK = 128
P_SIZE = 768


def per_device(anc_rows, row_home, block_lists, front_blocks, panel, pivot_inverse):
    groups = lax.axis_size("grp")
    pan_count = lax.axis_size("pan")
    group_idx = lax.axis_index("grp")
    pan_idx = lax.axis_index("pan")
    block_count = row_home.shape[0]
    front_len = block_lists.shape[1]
    rb_local = front_len // pan_count
    cb_local = anc_rows.shape[1] // BLK
    stored_blocks = anc_rows.shape[0] // BLK
    contract = (((0,), (0,)), ((), ()))
    my_list = lax.dynamic_index_in_dim(block_lists, group_idx, 0, keepdims=False)
    column_table = block_lists.reshape(groups, pan_count, rb_local)
    column_pick = (
        lax.dynamic_index_in_dim(column_table, pan_idx, 1, keepdims=False) - cb_local * pan_idx
    )
    slot_block = jnp.argsort(row_home)
    owned_slots = lax.dynamic_slice_in_dim(slot_block, group_idx * stored_blocks, stored_blocks)
    wanted = jnp.any(owned_slots[None, :, None] == block_lists[:, None, :], axis=2)
    layered = anc_rows.reshape(stored_blocks, BLK, cb_local, BLK)[:, :, column_pick, :]
    layered = jnp.transpose(layered, (2, 0, 1, 3, 4))
    layered = jnp.where(wanted[:, :, None, None, None], layered, jnp.zeros_like(layered))
    outgoing = layered.reshape(groups, stored_blocks * BLK, rb_local * BLK)
    received = lax.all_to_all(outgoing, "grp", split_axis=0, concat_axis=0, tiled=True)
    picked = received.reshape(block_count, BLK, rb_local * BLK)
    sigma_cols = picked[row_home[my_list]].reshape(front_len * BLK, rb_local * BLK)
    my_blocks = pan_idx * rb_local + jnp.arange(rb_local, dtype=jnp.int32)
    front_live = lax.dynamic_index_in_dim(front_blocks, group_idx, 0, keepdims=False)
    alive_rows = jnp.repeat(my_blocks < front_live, BLK)
    inverse_pivot = pivot_inverse[0]
    scaled = jnp.dot(panel[0], inverse_pivot, preferred_element_type=jnp.float32)
    scaled = jnp.where(alive_rows[:, None], scaled, jnp.zeros_like(scaled)).astype(jnp.bfloat16)
    product = lax.dot_general(
        sigma_cols,
        lax.all_gather(scaled, "pan", axis=0, tiled=True),
        contract,
        preferred_element_type=jnp.float32,
    )
    cross = jnp.where(alive_rows[:, None], -product, jnp.zeros_like(product)).astype(jnp.bfloat16)
    pivot_rows = P_SIZE // pan_count
    summed = lax.psum(
        (-lax.dot_general(scaled, cross, contract, preferred_element_type=jnp.float32)).astype(
            jnp.bfloat16
        ),
        "pan",
    ).astype(jnp.float32)
    shared = lax.dynamic_slice_in_dim(summed, pan_idx * pivot_rows, pivot_rows, 0)
    own_columns = lax.dynamic_slice_in_dim(inverse_pivot, pan_idx * pivot_rows, pivot_rows, 1)
    triangle = lax.dot_general(
        own_columns, inverse_pivot, contract, preferred_element_type=jnp.float32
    )
    pivot = triangle + shared
    return (cross[None], pivot[None])


def solution(mesh):
    placed = (P("grp", "pan"), P(), P(), P(), P("grp", "pan", None), P("grp", None, None))
    return jax.shard_map(
        per_device,
        mesh=mesh,
        in_specs=placed,
        out_specs=(P("grp", "pan", None), P("grp", "pan", None)),
        check_vma=False,
    )
```

profile of v0, /device:TPU:8, one launch (start us, length us, event | category | flops | bytes accessed | tf_op | source)
XLA Modules:
  0.0 340.6 jit_solution(7931357291125570440)
XLA Ops:
  7.2 0.0 copy-start
  7.2 0.0 all-gather.2.cloned.1.call-start
  7.2 1.3 dynamic_slice.23
  8.6 0.7 add_compare_fusion
  9.2 0.1 broadcast_bitcast_fusion
  9.3 0.0 copy-done
  9.3 2.2 fusion.1
  11.5 0.0 all-gather.2.cloned.1.call-update
  11.5 0.8 copy.19
  12.3 0.1 copy.20
  12.4 0.1 reshape.93
  12.5 4.0 %reshape.116 = bf16[16,128,4,128]{3,2,1,0:T(4,128)(2,1)} reshape(bf16[2048,512]{1,0:T(8,128)(2,1)} %param.6) | data formatting | bytes 4194304 | tf_op jit(solution)/shard_map/reshape | solution.py:29
  16.5 2.1 copy.21
  18.6 0.0 copy-start.1
  18.7 0.0 copy-start.4
  18.7 4.7 %gather_fusion = bf16[16,16,128,128]{3,2,1,0:T(8,128)(2,1)} fusion(bf16[16,128,4,128]{3,1,2,0:T(8,128)(2,1)S(1)} %copy.21, s32[1024]{0:T(1024)S(1)} %pad_clamp_fusion.2), kind=kCustom, calls=%fused_computation | custom fusion | bytes 16777280 | tf_op jit(solution)/shard_map/gather | solution.py:29
  23.4 2.5 sort.17
  25.9 0.1 dynamic_slice.24
  26.0 0.3 compare_reduce_fusion
  26.3 7.5 %select_bitcast_fusion = bf16[8,16,128,2,128]{4,2,1,3,0:T(8,128)(2,1)} fusion(bf16[8,2,16,128,128]{4,3,2,1,0:T(8,128)(2,1)} %bitcast.47, pred[8,16]{1,0:T(8,128)(4,1)S(1)} %compare_reduce_fusion), kind=kLoop, calls=%fused_computation.3 | loop fusion | flops 4194304 | bytes 16777344 | tf_op jit(solution)/shard_map/jit(_where)/select_n | solution.py:31
  33.8 16.4 %copy.22 = bf16[8,16,128,2,128]{4,3,2,1,0:T(2,128)(2,1)} copy(bf16[8,16,128,2,128]{4,2,1,3,0:T(8,128)(2,1)} %select_bitcast_fusion) | data formatting | bytes 16777216 | tf_op jit(solution)/shard_map/jit(_where)/select_n | solution.py:31
  50.2 14.1 %reshape.88 = bf16[8,2048,256]{2,1,0:T(8,128)(2,1)} reshape(bf16[8,16,128,2,128]{4,3,2,1,0:T(2,128)(2,1)} %copy.22) | data formatting | bytes 16777216 | tf_op jit(solution)/shard_map/reshape | solution.py:32
  64.3 7.2 %all-to-all-start = ((bf16[8,2048,256]{2,1,0:T(8,128)(2,1)}), bf16[8,2048,256]{2,1,0:T(8,128)(2,1)}, u32[]{:S(2)}, u32[]{:S(2)}) async-start(bf16[8,2048,256]{2,1,0:T(8,128)(2,1)} %reshape.88), calls=%async_computation | async-start | bytes 16777216 | tf_op jit(solution)/shard_map/all_to_all | solution.py:33
  71.5 0.8 gather_fusion.1
  72.3 92.5 %all-to-all-done = bf16[8,2048,256]{2,1,0:T(8,128)(2,1)} async-done(((bf16[8,2048,256]{2,1,0:T(8,128)(2,1)}), bf16[8,2048,256]{2,1,0:T(8,128)(2,1)}, u32[]{:S(2)}, u32[]{:S(2)}) %all-to-all-start) | async-done | bytes 8388640 | tf_op jit(solution)/shard_map/all_to_all | solution.py:33
  164.8 6.2 %gather_fusion.2 = bf16[64,128,256]{2,1,0:T(8,128)(2,1)} fusion(bf16[128,128,256]{2,1,0:T(8,128)(2,1)} %bitcast.6, s32[1024]{0:T(1024)S(1)} %pad_clamp_fusion), kind=kCustom, calls=%fused_computation.2 | custom fusion | bytes 8388864 | tf_op jit(solution)/shard_map/gather | solution.py:35
  171.0 9.3 %fusion.2 = bf16[256,768]{1,0:T(8,128)(2,1)S(1)} fusion(bf16[8192,256]{1,0:T(8,128)(2,1)} %bitcast.48, bf16[8192,768]{1,0:T(8,128)(2,1)} %all-gather.2.cloned.1.call-done, pred[256]{0:T(512)(128)(4,1)S(1)} %broadcast_bitcast_fusion), kind=kOutput, calls=%fused_computation.9 | convolution fusion | flops 3221815296 | bytes 17170688 | tf_op jit(solution)/shard_map/dot_general | solution.py:42
  180.3 0.0 copy-start.3
  180.3 1.6 negate_convert_fusion
  181.9 0.0 all-reduce.2.cloned.1.call-update
  181.9 150.1 %all-reduce.2.cloned.1.call-done = bf16[768,768]{1,0:T(8,128)(2,1)} async-done(((bf16[768,768]{1,0:T(8,128)(2,1)}), bf16[768,768]{1,0:T(8,128)(2,1)}) %all-reduce.2.cloned.1.call-update) | async-done | bytes 1179664 | tf_op jit(solution)/shard_map/psum | solution.py:50
  332.0 1.8 fusion.9
  (14 shorter events, 0.1 us)
Async XLA Ops:
  7.2 2.1 copy-start
  7.2 163.8 %all-gather.2.cloned.1.call-start = ((), (), s32[]{:S(2)}) async-start(), calls=%async_computation.1 | async-start | bytes 12976128 | tf_op jit(solution)/shard_map/all_gather | solution.py:44
  18.6 4.7 %copy-start.1 = (s32[128]{0:T(128)S(1)}, s32[128]{0:T(128)}, u32[]{:S(2)}) copy-start(s32[128]{0:T(128)} %param.7) | copy-start | bytes 1540
  18.7 7.3 %copy-start.4 = (s32[8,64]{1,0:T(8,128)S(1)}, s32[8,64]{1,0:T(8,128)}, u32[]{:S(2)}) copy-start(s32[8,64]{1,0:T(8,128)} %param.8) | copy-start | bytes 6148
  64.3 100.5 %all-to-all-start = ((bf16[8,2048,256]{2,1,0:T(8,128)(2,1)}), bf16[8,2048,256]{2,1,0:T(8,128)(2,1)}, u32[]{:S(2)}, u32[]{:S(2)}) async-start(bf16[8,2048,256]{2,1,0:T(8,128)(2,1)} %reshape.88), calls=%async_computation | async-start | bytes 16777216 | tf_op jit(solution)/shard_map/all_to_all | solution.py:33
  71.5 260.5 %all-reduce.2.cloned.1.call-start = ((), (), s32[]{:S(2)}) async-start(), calls=%async_computation.2 | async-start | bytes 2359296 | tf_op jit(solution)/shard_map/psum | solution.py:50
  171.0 9.3 %copy-start.2 = (bf16[256,768]{1,0:T(8,128)(2,1)S(1)}, bf16[256,768]{1,0:T(8,128)(2,1)}, u32[]{:S(2)}) copy-start(bf16[256,768]{1,0:T(8,128)(2,1)} %fusion.1) | copy-start | bytes 1179652
  180.3 153.5 %copy-start.3 = (bf16[256,768]{1,0:T(8,128)(2,1)}, bf16[256,768]{1,0:T(8,128)(2,1)S(1)}, u32[]{:S(2)}) copy-start(bf16[256,768]{1,0:T(8,128)(2,1)S(1)} %fusion.2) | copy-start | bytes 1179652
Sparse Core Ops, SparseCore 0:
  11.7 123.7 all-gather.1
  182.0 149.9 all-reduce.1
where the time goes:
time: 341 us
  waiting for transfers between devices  243 us (71%)
  local copies, waits for them, and re-layouts  50.8 us (15%)
  matrix products  14.9 us (4%)
  between operations  14.1 us (4%)
  other arithmetic  11 us (3%)
  starting transfers between devices  7.2 us (2%)
    psum x1, waiting for transfers between devices, per_device(): lax.psum((-lax.dot_general(scaled, cross, contract, preferred_element_typ...  150 us
    all_to_all x1, waiting for transfers between devices, per_device(): lax.all_to_all(outgoing, 'grp', split_axis=0, concat_axis=0, tiled=True)  92.5 us
    select_n x1, local copies, waits for them, and re-layouts, per_device(): jnp.where(wanted[:, :, None, None, None], layered, jnp.zeros_like(layered))  16.4 us
    reshape x1, local copies, waits for them, and re-layouts, per_device(): outgoing = layered.reshape(groups, stored_blocks * BLK, rb_local * BLK)  14.1 us
    dot_general x1, matrix products, per_device(): lax.dot_general(sigma_cols, lax.all_gather(scaled, 'pan', axis=0, tiled=T...  9.33 us
    select_n x1, other arithmetic, per_device(): jnp.where(wanted[:, :, None, None, None], layered, jnp.zeros_like(layered))  7.5 us
    all_to_all x1, starting transfers between devices, per_device(): lax.all_to_all(outgoing, 'grp', split_axis=0, concat_axis=0, tiled=True)  7.16 us
  transfers between devices with their start and end apart: 3, of which 2 were waited for; matrix products, arithmetic and copies ran while one was open for 18% of the time, Pallas kernels for 0%

commit v1 on v0

--- a/solution.py
+++ b/solution.py
@@ -47,11 +47,14 @@
     )
     cross = jnp.where(alive_rows[:, None], -product, jnp.zeros_like(product)).astype(jnp.bfloat16)
     pivot_rows = P_SIZE // pan_count
-    summed = lax.psum(
-        (-lax.dot_general(scaled, cross, contract, preferred_element_type=jnp.float32)).astype(
-            jnp.bfloat16
+    summed = jnp.sum(
+        lax.all_gather(
+            (-lax.dot_general(scaled, cross, contract, preferred_element_type=jnp.float32)).astype(
+                jnp.bfloat16
+            ),
+            "pan",
         ),
-        "pan",
+        axis=0,
     ).astype(jnp.float32)
     shared = lax.dynamic_slice_in_dim(summed, pan_idx * pivot_rows, pivot_rows, 0)
     own_columns = lax.dynamic_slice_in_dim(inverse_pivot, pan_idx * pivot_rows, pivot_rows, 1)

time: 341 us -> 462 us (1.35)
  waiting for transfers between devices: 243 us -> 351 us
  other arithmetic: 11 us -> 23.9 us
    all_gather x0 -> x1, waiting for transfers between devices: none -> 258 us  [per_device(): lax.all_gather((-lax.dot_general(scaled, cross, contract, preferred_eleme...]
    psum x1 -> x0, waiting for transfers between devices: 150 us -> none  [per_device(): lax.psum((-lax.dot_general(scaled, cross, contract, preferred_element_typ...]
    reduce_sum x0 -> x1, other arithmetic: none -> 12.9 us  [per_device(): jnp.sum(lax.all_gather((-lax.dot_general(scaled, cross, contract, preferr...]
  transfers between devices with their start and end apart: 3 -> 3, of which waited for: 2 -> 2; matrix products, arithmetic and copies ran while one was open for 18% -> 13% of each run, Pallas kernels for 0% -> 0%
where the time goes in v1:
time: 462 us; the launch traced here: 461 us
  waiting for transfers between devices  351 us (76%)
  local copies, waits for them, and re-layouts  50.8 us (11%)
  other arithmetic  23.9 us (5%)
  matrix products  14.1 us (3%)
  between operations  14.1 us (3%)
  starting transfers between devices  7.1 us (2%)
    all_gather x1, waiting for transfers between devices, per_device(): lax.all_gather((-lax.dot_general(scaled, cross, contract, preferred_eleme...  258 us
    all_to_all x1, waiting for transfers between devices, per_device(): lax.all_to_all(outgoing, 'grp', split_axis=0, concat_axis=0, tiled=True)  92.5 us
    select_n x1, local copies, waits for them, and re-layouts, per_device(): jnp.where(wanted[:, :, None, None, None], layered, jnp.zeros_like(layered))  16.4 us
    reshape x1, local copies, waits for them, and re-layouts, per_device(): outgoing = layered.reshape(groups, stored_blocks * BLK, rb_local * BLK)  14.1 us
    reduce_sum x1, other arithmetic, per_device(): jnp.sum(lax.all_gather((-lax.dot_general(scaled, cross, contract, preferr...  12.9 us
    dot_general x1, matrix products, per_device(): lax.dot_general(sigma_cols, lax.all_gather(scaled, 'pan', axis=0, tiled=T...  9.33 us
  transfers between devices with their start and end apart: 3, of which 2 were waited for; matrix products, arithmetic and copies ran while one was open for 13% of the time, Pallas kernels for 0%

profile of v1, /device:TPU:8, one launch (start us, length us, event | category | flops | bytes accessed | tf_op | source)
XLA Modules:
  0.0 460.8 jit_solution(8623421994079909479)
XLA Ops:
  7.2 0.0 copy-start
  7.2 0.0 all-gather.4.cloned.1.call-start
  7.2 1.3 dynamic_slice.23
  8.6 0.7 add_compare_fusion
  9.2 0.1 broadcast_bitcast_fusion
  9.3 0.0 copy-done
  9.3 2.2 fusion.1
  11.5 0.0 all-gather.4.cloned.1.call-update
  11.5 0.8 copy.19
  12.3 0.1 copy.20
  12.4 0.1 reshape.93
  12.5 4.0 reshape.117
  16.5 2.1 copy.21
  18.7 2.5 sort.17
  21.2 0.1 dynamic_slice.24
  21.3 4.7 %gather_fusion = bf16[16,16,128,128]{3,2,1,0:T(8,128)(2,1)} fusion(bf16[16,128,4,128]{3,1,2,0:T(8,128)(2,1)S(1)} %copy.21, s32[1024]{0:T(1024)S(1)} %pad_clamp_fusion.2), kind=kCustom, calls=%fused_computation | custom fusion | bytes 16777280 | tf_op jit(solution)/shard_map/gather | solution.py:29
  26.0 0.3 compare_reduce_fusion
  26.3 7.5 %select_bitcast_fusion = bf16[8,16,128,2,128]{4,2,1,3,0:T(8,128)(2,1)} fusion(bf16[8,2,16,128,128]{4,3,2,1,0:T(8,128)(2,1)} %bitcast.49, pred[8,16]{1,0:T(8,128)(4,1)S(1)} %compare_reduce_fusion), kind=kLoop, calls=%fused_computation.3 | loop fusion | flops 4194304 | bytes 16777344 | tf_op jit(solution)/shard_map/jit(_where)/select_n | solution.py:31
  33.8 16.4 %copy.22 = bf16[8,16,128,2,128]{4,3,2,1,0:T(2,128)(2,1)} copy(bf16[8,16,128,2,128]{4,2,1,3,0:T(8,128)(2,1)} %select_bitcast_fusion) | data formatting | bytes 16777216 | tf_op jit(solution)/shard_map/jit(_where)/select_n | solution.py:31
  50.2 14.1 %reshape.88 = bf16[8,2048,256]{2,1,0:T(8,128)(2,1)} reshape(bf16[8,16,128,2,128]{4,3,2,1,0:T(2,128)(2,1)} %copy.22) | data formatting | bytes 16777216 | tf_op jit(solution)/shard_map/reshape | solution.py:32
  64.3 7.1 %all-to-all-start = ((bf16[8,2048,256]{2,1,0:T(8,128)(2,1)}), bf16[8,2048,256]{2,1,0:T(8,128)(2,1)}, u32[]{:S(2)}, u32[]{:S(2)}) async-start(bf16[8,2048,256]{2,1,0:T(8,128)(2,1)} %reshape.88), calls=%async_computation | async-start | bytes 16777216 | tf_op jit(solution)/shard_map/all_to_all | solution.py:33
  71.4 0.8 gather_fusion.1
  72.2 92.5 %all-to-all-done = bf16[8,2048,256]{2,1,0:T(8,128)(2,1)} async-done(((bf16[8,2048,256]{2,1,0:T(8,128)(2,1)}), bf16[8,2048,256]{2,1,0:T(8,128)(2,1)}, u32[]{:S(2)}, u32[]{:S(2)}) %all-to-all-start) | async-done | bytes 8388640 | tf_op jit(solution)/shard_map/all_to_all | solution.py:33
  164.7 6.2 %gather_fusion.2 = bf16[64,128,256]{2,1,0:T(8,128)(2,1)} fusion(bf16[128,128,256]{2,1,0:T(8,128)(2,1)} %bitcast.6, s32[1024]{0:T(1024)S(1)} %pad_clamp_fusion), kind=kCustom, calls=%fused_computation.2 | custom fusion | bytes 8388864 | tf_op jit(solution)/shard_map/gather | solution.py:35
  170.8 9.3 %fusion.2 = bf16[256,768]{1,0:T(8,128)(2,1)S(1)} fusion(bf16[8192,256]{1,0:T(8,128)(2,1)} %bitcast.50, bf16[8192,768]{1,0:T(8,128)(2,1)} %all-gather.4.cloned.1.call-done, pred[256]{0:T(512)(128)(4,1)S(1)} %broadcast_bitcast_fusion), kind=kOutput, calls=%fused_computation.9 | convolution fusion | flops 3221815296 | bytes 17170688 | tf_op jit(solution)/shard_map/dot_general | solution.py:42
  180.2 0.0 copy-start.3
  180.2 1.5 negate_convert_fusion
  181.8 0.0 all-gather.6.cloned.1.call-update
  181.8 258.2 %all-gather.6.cloned.1.call-done = bf16[24576,768]{1,0:T(8,128)(2,1)} async-done(((bf16[768,768]{1,0:T(8,128)(2,1)}), bf16[24576,768]{1,0:T(8,128)(2,1)}) %all-gather.6.cloned.1.call-update) | async-done | bytes 37748752 | tf_op jit(solution)/shard_map/all_gather | solution.py:51
  440.0 12.9 %reduce_sum.12 = bf16[768,768]{1,0:T(8,128)(2,1)S(1)} reduce(bf16[32,768,768]{2,1,0:T(8,128)(2,1)} %bitcast.48, bf16[]{:T(256)} %constant.26.clone.1), dimensions={0}, to_apply=%region_2.3 | reduce | flops 18284544 | bytes 38928384 | tf_op jit(solution)/shard_map/reduce_sum | solution.py:50
  452.9 0.0 copy-done.3
  453.0 1.0 fusion.9
  (15 shorter events, 0.1 us)
Async XLA Ops:
  7.2 2.1 copy-start
  7.2 163.7 %all-gather.4.cloned.1.call-start = ((), (), s32[]{:S(2)}) async-start(), calls=%async_computation.1 | async-start | bytes 12976128 | tf_op jit(solution)/shard_map/all_gather | solution.py:44
  12.5 6.2 %copy-start.1 = (s32[128]{0:T(128)S(1)}, s32[128]{0:T(128)}, u32[]{:S(2)}) copy-start(s32[128]{0:T(128)} %param.7) | copy-start | bytes 1540
  21.3 4.7 %copy-start.4 = (s32[8,64]{1,0:T(8,128)S(1)}, s32[8,64]{1,0:T(8,128)}, u32[]{:S(2)}) copy-start(s32[8,64]{1,0:T(8,128)} %param.8) | copy-start | bytes 6148
  64.3 100.4 %all-to-all-start = ((bf16[8,2048,256]{2,1,0:T(8,128)(2,1)}), bf16[8,2048,256]{2,1,0:T(8,128)(2,1)}, u32[]{:S(2)}, u32[]{:S(2)}) async-start(bf16[8,2048,256]{2,1,0:T(8,128)(2,1)} %reshape.88), calls=%async_computation | async-start | bytes 16777216 | tf_op jit(solution)/shard_map/all_to_all | solution.py:33
  71.4 368.6 %all-gather.6.cloned.1.call-start = ((), (), s32[]{:S(2)}) async-start(), calls=%async_computation.2 | async-start | bytes 38928384 | tf_op jit(solution)/shard_map/all_gather | solution.py:51
  170.8 9.3 %copy-start.2 = (bf16[256,768]{1,0:T(8,128)(2,1)S(1)}, bf16[256,768]{1,0:T(8,128)(2,1)}, u32[]{:S(2)}) copy-start(bf16[256,768]{1,0:T(8,128)(2,1)} %fusion.1) | copy-start | bytes 1179652
  180.2 272.8 %copy-start.3 = (bf16[256,768]{1,0:T(8,128)(2,1)}, bf16[256,768]{1,0:T(8,128)(2,1)S(1)}, u32[]{:S(2)}) copy-start(bf16[256,768]{1,0:T(8,128)(2,1)S(1)} %fusion.2) | copy-start | bytes 1179652
Sparse Core Ops, SparseCore 0:
  11.7 122.4 all-gather.3
  181.9 258.0 all-gather.5
